TPU v7x, 32 devices: a whole 2x2x4 slice. The times are simulated.
32 devices in a mesh: rows: 4 (over x, core), feat: 8 (over z, y).
Axes of the slice: x: 2, y: 2, z: 4, core: 2. Of those that a mesh axis runs over, the one named last changes fastest.
Arguments:
- embeddings: bfloat16 [512, 1024], P(('rows', 'feat')), may hold values from -12 to 12
- freqs: bfloat16 [1024, 65536], P(None, 'feat'), may hold values from -0.1875 to 0.1875
- phases: float32 [65536], P('feat'), may hold values from 0 to 6.2831855
- sketch: bfloat16 [65536, 256], P('feat'), may hold values from -0.0234375 to 0.0234375
Outputs:
- basis: float32 [512, 256], P(('rows', 'feat'))
- coeffs: float32 [256, 65536], P(None, 'feat')
All inputs are finite; a program needn't handle non-finite values.
Results may differ from a plain program's by a relative error of at most 0.0048.
Values may be sent and summed in bfloat16 or wider, within the bound.
A program may use at most 128 MiB of HBM per device.

v0:
```python
import jax
import jax.numpy as jnp
from jax import lax
from jax.sharding import PartitionSpec as P


def per_device(embeddings, freqs, phases, sketch):
    rows_dev = embeddings.shape[0]
    row_count = rows_dev * lax.axis_size("feat") * lax.axis_size("rows")
    mixed = jnp.dot(
        lax.all_gather(embeddings, "feat", axis=0, tiled=True),
        freqs,
        preferred_element_type=jnp.float32,
    )
    features = jnp.cos(mixed + phases).astype(jnp.bfloat16)
    owned_rows = lax.psum_scatter(
        jnp.dot(features, sketch, preferred_element_type=jnp.float32),
        "feat",
        scatter_dimension=0,
        tiled=True,
    )
    local_gram = jnp.dot(owned_rows.T, owned_rows, precision=lax.Precision.HIGHEST)
    gram_matrix = lax.psum(local_gram, ("rows", "feat")) / row_count
    factor = jnp.linalg.cholesky(gram_matrix)
    basis = jax.scipy.linalg.solve_triangular(factor, owned_rows.T, lower=True).T
    block_basis = lax.all_gather(basis.astype(jnp.bfloat16), "feat", axis=0, tiled=True)
    partial_value = lax.dot_general(
        block_basis, features, (((0,), (0,)), ((), ())), preferred_element_type=jnp.float32
    )
    coeffs = lax.psum(partial_value, "rows") / row_count
    return (basis, coeffs)


def solution(mesh):
    placed = (P(("rows", "feat"), None), P(None, "feat"), P("feat"), P("feat", None))
    return jax.shard_map(
        per_device,
        mesh=mesh,
        in_specs=placed,
        out_specs=(P(("rows", "feat"), None), P(None, "feat")),
        check_vma=False,
    )
```

profile of v0, /device:TPU:0, one launch (start us, length us, event | category | flops | bytes accessed | tf_op | source)
XLA Modules:
  0.0 516.5 jit_solution(3243274491165157878)
XLA Ops:
  7.2 32.7 %all_gather.6 = bf16[128,1024]{1,0:T(8,128)(2,1)S(1)} all-gather(bf16[16,1024]{1,0:T(8,128)(2,1)} %param.4), channel_id=1, replica_groups=mesh['rows'=4,'feat'=8] {'feat'}, dimensions={0}, use_global_device_ids=true | all-gather | bytes 294912 | tf_op jit(solution)/shard_map/all_gather | solution.py:11
  40.0 18.1 %fusion.1 = bf16[128,8192]{1,0:T(8,128)(2,1)S(1)} fusion(bf16[128,1024]{1,0:T(8,128)(2,1)S(1)} %all_gather.6, bf16[1024,8192]{1,0:T(8,128)(2,1)} %param.5, f32[8192]{0:T(1024)} %param.6), kind=kOutput, calls=%fused_computation.4 | convolution fusion | flops 2149580800 | bytes 19169280 | tf_op jit(solution)/shard_map/dot_general | solution.py:10
  58.1 1.5 fusion.12
  59.6 0.0 all-reduce.4.cloned.1.call-start
  59.6 62.0 %reduce-scatter.2.cloned.1.call-done = f32[16,256]{1,0:T(8,128)} async-done(((f32[128,256]{1,0:T(8,128)}), f32[16,256]{1,0:T(8,128)}) %reduce-scatter.2.cloned.1.call-update) | async-done | bytes 16400 | tf_op jit(solution)/shard_map/reduce_scatter | solution.py:16
  121.6 1.9 fusion.13
  123.6 0.2 all-reduce.6.cloned.1.call-start
  123.8 128.0 %all-reduce.4.cloned.1.call-done = f32[256,256]{0,1:T(8,128)} async-done(((f32[256,256]{0,1:T(8,128)}), f32[256,256]{0,1:T(8,128)}) %all-reduce.4.cloned.1.call-update) | async-done | bytes 262160 | tf_op jit(solution)/shard_map/psum | solution.py:23
  251.8 1.0 broadcast_multiply_fusion.1
  252.8 0.1 copy.7
  252.9 1.0 fusion.2
  253.9 11.7 %cholesky.50 = f32[128,128]{1,0:T(8,128)S(1)} custom-call(f32[128,128]{1,0:T(8,128)S(1)} %cholesky.118), custom_call_target="Cholesky" | custom-call | tf_op jit(solution)/shard_map/jit(cholesky)/cholesky | solution.py:24
  265.7 9.8 %custom-call.15 = f32[1,128,128]{1,2,0:T(8,128)S(1)} custom-call(f32[1,128,128]{2,1,0:T(8,128)S(1)} %get-tuple-element.25), custom_call_target="InvertDiagBlocksLowerTriangular" | custom-call | tf_op jit(solution)/shard_map/jit(cholesky)/cholesky | solution.py:24
  275.5 0.2 constant_dynamic-update-slice_fusion.1
  275.7 0.3 convolution_subtract_fusion
  276.0 11.7 %cholesky.105 = f32[128,128]{1,0:T(8,128)S(1)} custom-call(f32[128,128]{1,0:T(8,128)S(1)} %convolution_subtract_fusion), custom_call_target="Cholesky" | custom-call | tf_op jit(solution)/shard_map/jit(cholesky)/cholesky | solution.py:24
  287.8 0.7 compare_reduce_fusion
  289.9 0.1 triangular_solve.57
  289.9 4.3 while.1
  290.1 0.6 fusion.28
  290.7 1.4 bitcast_dynamic-update-slice_fusion.2
  292.2 0.6 fusion.28
  292.8 1.4 bitcast_dynamic-update-slice_fusion.2
  294.2 19.7 %custom-call.16 = f32[2,128,128]{1,2,0:T(8,128)S(1)} custom-call(f32[2,128,128]{2,1,0:T(8,128)S(1)} %get-tuple-element.9), custom_call_target="InvertDiagBlocksLowerTriangular" | custom-call | tf_op jit(solution)/shard_map/jit(_solve_triangular)/triangular_solve | solution.py:25
  313.9 0.2 fusion.5
  314.1 0.2 convolution_subtract_fusion.1
  314.3 0.2 fusion.4
  314.5 0.6 fusion.10
  315.1 30.5 %all_gather.7 = bf16[128,256]{1,0:T(8,128)(2,1)S(1)} all-gather(bf16[16,256]{1,0:T(8,128)(2,1)S(1)} %get-tuple-element.18), channel_id=1, replica_groups=mesh['rows'=4,'feat'=8] {'feat'}, dimensions={0}, use_global_device_ids=true | all-gather | bytes 73728 | tf_op jit(solution)/shard_map/all_gather | solution.py:26
  345.6 4.7 fusion.14
  350.3 152.0 %all-reduce.6.cloned.1.call-done = f32[256,8192]{1,0:T(8,128)} async-done(((f32[256,8192]{1,0:T(8,128)}), f32[256,8192]{1,0:T(8,128)}) %all-reduce.6.cloned.1.call-update) | async-done | bytes 8388624 | tf_op jit(solution)/shard_map/psum | solution.py:30
  502.3 7.7 %broadcast_multiply_fusion = f32[256,8192]{1,0:T(8,128)} fusion(f32[256,8192]{1,0:T(8,128)} %all-reduce.6.cloned.1.call-done), kind=kLoop, calls=%fused_computation.5 | loop fusion | flops 2097152 | bytes 16777216 | tf_op jit(solution)/shard_map/div | solution.py:30
  (17 shorter events, 0.2 us)
Async XLA Ops:
  7.2 114.5 %reduce-scatter.2.cloned.1.call-start = ((), (), s32[]{:S(2)}) async-start(), calls=%async_computation.1 | async-start | bytes 147456 | tf_op jit(solution)/shard_map/reduce_scatter | solution.py:16
  39.9 18.2 %copy-start = (bf16[8192,256]{1,0:T(8,128)(2,1)S(1)}, bf16[8192,256]{1,0:T(8,128)(2,1)}, u32[]{:S(2)}) copy-start(bf16[8192,256]{1,0:T(8,128)(2,1)} %param.7) | copy-start | bytes 12582916
  59.6 192.2 %all-reduce.4.cloned.1.call-start = ((), (), s32[]{:S(2)}) async-start(), calls=%async_computation.2 | async-start | bytes 524288 | tf_op jit(solution)/shard_map/psum | solution.py:23
  121.6 192.3 %copy-start.1 = (f32[16,256]{1,0:T(8,128)S(1)}, f32[16,256]{1,0:T(8,128)}, u32[]{:S(2)}) copy-start(f32[16,256]{1,0:T(8,128)} %reduce-scatter.2.cloned.1.call-done) | copy-start | bytes 49156
  123.6 378.7 %all-reduce.6.cloned.1.call-start = ((), (), s32[]{:S(2)}) async-start(), calls=%async_computation.3 | async-start | bytes 16777216 | tf_op jit(solution)/shard_map/psum | solution.py:30
Sparse Core Ops, SparseCore 0:
  59.7 61.8 reduce-scatter.1
  127.7 124.0 all-reduce.3
  350.4 151.8 all-reduce.5
where the time goes:
time: 517 us
  waiting for transfers between devices  342 us (66%)
  other arithmetic  64 us (12%)
  blocking collectives  63.2 us (12%)
  matrix products  27.2 us (5%)
  between operations  15.2 us (3%)
    psum x1, waiting for transfers between devices, per_device(): coeffs = lax.psum(partial_value, 'rows') / row_count  152 us
    psum x1, waiting for transfers between devices, per_device(): gram_matrix = lax.psum(local_gram, ('rows', 'feat')) / row_count  128 us
    reduce_scatter x1, waiting for transfers between devices, per_device(): lax.psum_scatter(jnp.dot(features, sketch, preferred_element_type=jnp.flo...  62 us
    another operation x6, other arithmetic, per_device(): factor = jnp.linalg.cholesky(gram_matrix)  34 us
    all_gather x1, blocking collectives, per_device(): lax.all_gather(embeddings, 'feat', axis=0, tiled=True)  32.7 us
    all_gather x1, blocking collectives, per_device(): lax.all_gather(basis.astype(jnp.bfloat16), 'feat', axis=0, tiled=True)  30.5 us
    another operation x3, other arithmetic, per_device(): jax.scipy.linalg.solve_triangular(factor, owned_rows.T, lower=True)  19.7 us
    dot_general x1, matrix products, per_device(): jnp.dot(lax.all_gather(embeddings, 'feat', axis=0, tiled=True), freqs, pr...  18.1 us
  transfers between devices with their start and end apart: 3, of which 3 were waited for; matrix products, arithmetic and copies ran while one was open for 0% of the time, Pallas kernels for 0%

commit v1 on v0

--- a/solution.py
+++ b/solution.py
@@ -4,14 +4,28 @@
 from jax.sharding import PartitionSpec as P
 
 
+def collect(value, axis, dim):
+    ways, here, hop = (lax.axis_size(axis), lax.axis_index(axis), value.shape[dim])
+    shape = [n * ways if d == dim else n for d, n in enumerate(value.shape)]
+    full = lax.dynamic_update_slice_in_dim(
+        jnp.zeros(shape, value.dtype), value, here * hop, axis=dim
+    )
+    going_up = going_down = value
+    for far in range(1, ways // 2 + 1):
+        going_up = lax.ppermute(going_up, axis, [(d, (d + 1) % ways) for d in range(ways)])
+        full = lax.dynamic_update_slice_in_dim(full, going_up, (here - far) % ways * hop, axis=dim)
+        if 2 * far < ways:
+            going_down = lax.ppermute(going_down, axis, [(d, (d - 1) % ways) for d in range(ways)])
+            full = lax.dynamic_update_slice_in_dim(
+                full, going_down, (here + far) % ways * hop, axis=dim
+            )
+    return full
+
+
 def per_device(embeddings, freqs, phases, sketch):
     rows_dev = embeddings.shape[0]
     row_count = rows_dev * lax.axis_size("feat") * lax.axis_size("rows")
-    mixed = jnp.dot(
-        lax.all_gather(embeddings, "feat", axis=0, tiled=True),
-        freqs,
-        preferred_element_type=jnp.float32,
-    )
+    mixed = jnp.dot(collect(embeddings, "feat", 0), freqs, preferred_element_type=jnp.float32)
     features = jnp.cos(mixed + phases).astype(jnp.bfloat16)
     owned_rows = lax.psum_scatter(
         jnp.dot(features, sketch, preferred_element_type=jnp.float32),

time: 517 us -> 513 us (level)
  blocking collectives: 63.2 us -> 30.5 us
  starting transfers between devices: 0.3 us -> 16.3 us
  waiting for transfers between devices: 342 us -> 354 us
    all_gather x1 -> x0, blocking collectives: 32.7 us -> none  [per_device(): lax.all_gather(embeddings, 'feat', axis=0, tiled=True)]
    ppermute x0 -> x7, starting transfers between devices: none -> 16 us  [the longest x3 16 us: collect(): lax.ppermute(going_down, axis, [(d, (d - 1) % ways) for d in range(ways)])]
    ppermute x0 -> x7, waiting for transfers between devices: none -> 15.8 us  [the longest x4 13.2 us: collect(): lax.ppermute(going_up, axis, [(d, (d + 1) % ways) for d in range(ways)])]
  transfers between devices with their start and end apart: 3 -> 10, of which waited for: 3 -> 7; matrix products, arithmetic and copies ran while one was open for 0% -> 0% of each run, Pallas kernels for 0% -> 0%
where the time goes in v1:
time: 513 us; the launch traced here: 512 us
  waiting for transfers between devices  354 us (69%)
  other arithmetic  64 us (12%)
  blocking collectives  30.5 us (6%)
  matrix products  27.2 us (5%)
  starting transfers between devices  16.3 us (3%)
  between operations  15.2 us (3%)
    psum x1, waiting for transfers between devices, per_device(): coeffs = lax.psum(partial_value, 'rows') / row_count  152 us
    psum x1, waiting for transfers between devices, per_device(): gram_matrix = lax.psum(local_gram, ('rows', 'feat')) / row_count  128 us
    reduce_scatter x1, waiting for transfers between devices, per_device(): lax.psum_scatter(jnp.dot(features, sketch, preferred_element_type=jnp.flo...  58.3 us
    another operation x6, other arithmetic, per_device(): factor = jnp.linalg.cholesky(gram_matrix)  34 us
    all_gather x1, blocking collectives, per_device(): lax.all_gather(basis.astype(jnp.bfloat16), 'feat', axis=0, tiled=True)  30.5 us
    another operation x3, other arithmetic, per_device(): jax.scipy.linalg.solve_triangular(factor, owned_rows.T, lower=True)  19.7 us
    dot_general x1, matrix products, per_device(): jnp.dot(collect(embeddings, 'feat', 0), freqs, preferred_element_type=jnp...  18.1 us
    ppermute x3, starting transfers between devices, collect(): lax.ppermute(going_down, axis, [(d, (d - 1) % ways) for d in range(ways)])  16 us
  transfers between devices with their start and end apart: 10, of which 7 were waited for; matrix products, arithmetic and copies ran while one was open for 0% of the time, Pallas kernels for 0%

profile of v1, /device:TPU:0, one launch (start us, length us, event | category | flops | bytes accessed | tf_op | source)
XLA Modules:
  0.0 512.4 jit_solution(13264872398807829216)
XLA Ops:
  7.2 6.1 %collective-permute-start.1 = (bf16[16,1024]{1,0:T(8,128)(2,1)}, bf16[16,1024]{1,0:T(8,128)(2,1)S(1)}, u32[]{:S(2)}, u32[]{:S(2)}) collective-permute-start(bf16[16,1024]{1,0:T(8,128)(2,1)} %param.4), channel_id=1, source_target_pairs={{0,7},{1,0},{2,1},{3,2},{4,3},{5,4},{6,5},{7,6},{8,15},{9,8},{10,9... | collective-permute-start | bytes 98312 | tf_op jit(solution)/shard_map/ppermute | solution.py:18
  13.3 0.8 constant_dynamic-update-slice_fusion.8
  14.1 1.1 collective-permute-done.1
  15.2 4.9 collective-permute-start.3
  20.1 1.6 collective-permute-done.3
  21.7 5.0 collective-permute-start.5
  26.7 6.6 %collective-permute-done.4 = bf16[16,1024]{1,0:T(8,128)(2,1)S(1)} collective-permute-done((bf16[16,1024]{1,0:T(8,128)(2,1)S(1)}, bf16[16,1024]{1,0:T(8,128)(2,1)S(1)}, u32[]{:S(2)}, u32[]{:S(2)}) %collective-permute-start.4) | collective-permute-done | bytes 32800 | tf_op jit(solution)/shard_map/ppermute | solution.py:15
  33.4 6.6 %collective-permute-done.6 = bf16[16,1024]{1,0:T(8,128)(2,1)S(1)} collective-permute-done((bf16[16,1024]{1,0:T(8,128)(2,1)S(1)}, bf16[16,1024]{1,0:T(8,128)(2,1)S(1)}, u32[]{:S(2)}, u32[]{:S(2)}) %collective-permute-start.6) | collective-permute-done | bytes 32800 | tf_op jit(solution)/shard_map/ppermute | solution.py:15
  39.9 18.1 %fusion.1 = bf16[128,8192]{1,0:T(8,128)(2,1)S(1)} fusion(bf16[128,1024]{1,0:T(8,128)(2,1)S(1)} %constant_dynamic-update-slice_fusion.1, bf16[1024,8192]{1,0:T(8,128)(2,1)} %param.5, f32[8192]{0:T(1024)} %param.6), kind=kOutput, calls=%fused_computation.4 | convolution fusion | flops 2149580800 | bytes 19169280 | tf_op jit(solution)/shard_map/dot_general | solution.py:28
  58.1 1.5 fusion.12
  59.6 58.3 %reduce-scatter.2.cloned.1.call-done = f32[16,256]{1,0:T(8,128)} async-done(((f32[128,256]{1,0:T(8,128)}), f32[16,256]{1,0:T(8,128)}) %reduce-scatter.2.cloned.1.call-update) | async-done | bytes 16400 | tf_op jit(solution)/shard_map/reduce_scatter | solution.py:30
  117.9 1.9 fusion.13
  119.9 0.2 all-reduce.6.cloned.1.call-start
  120.1 127.9 %all-reduce.4.cloned.1.call-done = f32[256,256]{0,1:T(8,128)} async-done(((f32[256,256]{0,1:T(8,128)}), f32[256,256]{0,1:T(8,128)}) %all-reduce.4.cloned.1.call-update) | async-done | bytes 262160 | tf_op jit(solution)/shard_map/psum | solution.py:37
  248.0 1.0 broadcast_multiply_fusion.1
  249.1 1.0 fusion.2
  250.1 11.7 %cholesky.50 = f32[128,128]{1,0:T(8,128)S(1)} custom-call(f32[128,128]{1,0:T(8,128)S(1)} %cholesky.118), custom_call_target="Cholesky" | custom-call | tf_op jit(solution)/shard_map/jit(cholesky)/cholesky | solution.py:38
  261.9 9.8 %custom-call.15 = f32[1,128,128]{1,2,0:T(8,128)S(1)} custom-call(f32[1,128,128]{2,1,0:T(8,128)S(1)} %get-tuple-element.25), custom_call_target="InvertDiagBlocksLowerTriangular" | custom-call | tf_op jit(solution)/shard_map/jit(cholesky)/cholesky | solution.py:38
  271.9 0.3 convolution_subtract_fusion
  272.2 11.7 %cholesky.105 = f32[128,128]{1,0:T(8,128)S(1)} custom-call(f32[128,128]{1,0:T(8,128)S(1)} %convolution_subtract_fusion), custom_call_target="Cholesky" | custom-call | tf_op jit(solution)/shard_map/jit(cholesky)/cholesky | solution.py:38
  283.9 0.7 compare_reduce_fusion
  286.0 4.1 while.1
  286.2 0.6 fusion.28
  286.8 1.4 bitcast_dynamic-update-slice_fusion.2
  288.1 0.6 fusion.28
  288.7 1.4 bitcast_dynamic-update-slice_fusion.2
  290.1 19.7 %custom-call.16 = f32[2,128,128]{1,2,0:T(8,128)S(1)} custom-call(f32[2,128,128]{2,1,0:T(8,128)S(1)} %get-tuple-element.9), custom_call_target="InvertDiagBlocksLowerTriangular" | custom-call | tf_op jit(solution)/shard_map/jit(_solve_triangular)/triangular_solve | solution.py:39
  310.3 0.6 fusion.10
  311.0 30.5 %all_gather.3 = bf16[128,256]{1,0:T(8,128)(2,1)S(1)} all-gather(bf16[16,256]{1,0:T(8,128)(2,1)S(1)} %get-tuple-element.18), channel_id=1, replica_groups=mesh['rows'=4,'feat'=8] {'feat'}, dimensions={0}, use_global_device_ids=true | all-gather | bytes 73728 | tf_op jit(solution)/shard_map/all_gather | solution.py:40
  341.5 4.7 fusion.14
  346.2 152.0 %all-reduce.6.cloned.1.call-done = f32[256,8192]{1,0:T(8,128)} async-done(((f32[256,8192]{1,0:T(8,128)}), f32[256,8192]{1,0:T(8,128)}) %all-reduce.6.cloned.1.call-update) | async-done | bytes 8388624 | tf_op jit(solution)/shard_map/psum | solution.py:44
  498.2 7.7 %broadcast_multiply_fusion = f32[256,8192]{1,0:T(8,128)} fusion(f32[256,8192]{1,0:T(8,128)} %all-reduce.6.cloned.1.call-done), kind=kLoop, calls=%fused_computation.5 | loop fusion | flops 2097152 | bytes 16777216 | tf_op jit(solution)/shard_map/div | solution.py:44
  (39 shorter events, 1.3 us)
Async XLA Ops:
  7.2 110.7 %reduce-scatter.2.cloned.1.call-start = ((), (), s32[]{:S(2)}) async-start(), calls=%async_computation.1 | async-start | bytes 147456 | tf_op jit(solution)/shard_map/reduce_scatter | solution.py:30
  7.2 8.0 %collective-permute-start.1 = (bf16[16,1024]{1,0:T(8,128)(2,1)}, bf16[16,1024]{1,0:T(8,128)(2,1)S(1)}, u32[]{:S(2)}, u32[]{:S(2)}) collective-permute-start(bf16[16,1024]{1,0:T(8,128)(2,1)} %param.4), channel_id=1, source_target_pairs={{0,7},{1,0},{2,1},{3,2},{4,3},{5,4},{6,5},{7,6},{8,15},{9,8},{10,9... | collective-permute-start | bytes 98312 | tf_op jit(solution)/shard_map/ppermute | solution.py:18
  13.3 6.8 %collective-permute-start = (bf16[16,1024]{1,0:T(8,128)(2,1)}, bf16[16,1024]{1,0:T(8,128)(2,1)S(1)}, u32[]{:S(2)}, u32[]{:S(2)}) collective-permute-start(bf16[16,1024]{1,0:T(8,128)(2,1)} %param.4), channel_id=1, source_target_pairs={{0,1},{1,2},{2,3},{3,4},{4,5},{5,6},{6,7},{7,0},{8,9},{9,10},{10,1... | collective-permute-start | bytes 98312 | tf_op jit(solution)/shard_map/ppermute | solution.py:15
  15.2 6.5 %collective-permute-start.3 = (bf16[16,1024]{1,0:T(8,128)(2,1)S(1)}, bf16[16,1024]{1,0:T(8,128)(2,1)S(1)}, u32[]{:S(2)}, u32[]{:S(2)}) collective-permute-start(bf16[16,1024]{1,0:T(8,128)(2,1)S(1)} %collective-permute-done.1), channel_id=1, source_target_pairs={{0,7},{1,0},{2,1},{3,2},{4,3},{5,4},{6,5},{7,6},{8,15},{9,8},{10,9... | collective-permute-start | bytes 98312 | tf_op jit(solution)/shard_map/ppermute | solution.py:18
  20.1 6.6 %collective-permute-start.2 = (bf16[16,1024]{1,0:T(8,128)(2,1)S(1)}, bf16[16,1024]{1,0:T(8,128)(2,1)S(1)}, u32[]{:S(2)}, u32[]{:S(2)}) collective-permute-start(bf16[16,1024]{1,0:T(8,128)(2,1)S(1)} %collective-permute-done), channel_id=1, source_target_pairs={{0,1},{1,2},{2,3},{3,4},{4,5},{5,6},{6,7},{7,0},{8,9},{9,10},{10,1... | collective-permute-start | bytes 98312 | tf_op jit(solution)/shard_map/ppermute | solution.py:15
  21.7 11.6 %collective-permute-start.5 = (bf16[16,1024]{1,0:T(8,128)(2,1)S(1)}, bf16[16,1024]{1,0:T(8,128)(2,1)S(1)}, u32[]{:S(2)}, u32[]{:S(2)}) collective-permute-start(bf16[16,1024]{1,0:T(8,128)(2,1)S(1)} %collective-permute-done.3), channel_id=1, source_target_pairs={{0,7},{1,0},{2,1},{3,2},{4,3},{5,4},{6,5},{7,6},{8,15},{9,8},{10,9... | collective-permute-start | bytes 98312 | tf_op jit(solution)/shard_map/ppermute | solution.py:18
  26.7 6.6 %collective-permute-start.4 = (bf16[16,1024]{1,0:T(8,128)(2,1)S(1)}, bf16[16,1024]{1,0:T(8,128)(2,1)S(1)}, u32[]{:S(2)}, u32[]{:S(2)}) collective-permute-start(bf16[16,1024]{1,0:T(8,128)(2,1)S(1)} %collective-permute-done.2), channel_id=1, source_target_pairs={{0,1},{1,2},{2,3},{3,4},{4,5},{5,6},{6,7},{7,0},{8,9},{9,10},{10,1... | collective-permute-start | bytes 98312 | tf_op jit(solution)/shard_map/ppermute | solution.py:15
  33.3 6.6 %collective-permute-start.6 = (bf16[16,1024]{1,0:T(8,128)(2,1)S(1)}, bf16[16,1024]{1,0:T(8,128)(2,1)S(1)}, u32[]{:S(2)}, u32[]{:S(2)}) collective-permute-start(bf16[16,1024]{1,0:T(8,128)(2,1)S(1)} %collective-permute-done.4), channel_id=1, source_target_pairs={{0,1},{1,2},{2,3},{3,4},{4,5},{5,6},{6,7},{7,0},{8,9},{9,10},{10,1... | collective-permute-start | bytes 98312 | tf_op jit(solution)/shard_map/ppermute | solution.py:15
  39.9 18.2 %copy-start = (bf16[8192,256]{1,0:T(8,128)(2,1)S(1)}, bf16[8192,256]{1,0:T(8,128)(2,1)}, u32[]{:S(2)}) copy-start(bf16[8192,256]{1,0:T(8,128)(2,1)} %param.7) | copy-start | bytes 12582916
  59.6 188.4 %all-reduce.4.cloned.1.call-start = ((), (), s32[]{:S(2)}) async-start(), calls=%async_computation.2 | async-start | bytes 524288 | tf_op jit(solution)/shard_map/psum | solution.py:37
  117.9 191.9 %copy-start.1 = (f32[16,256]{1,0:T(8,128)S(1)}, f32[16,256]{1,0:T(8,128)}, u32[]{:S(2)}) copy-start(f32[16,256]{1,0:T(8,128)} %reduce-scatter.2.cloned.1.call-done) | copy-start | bytes 49156
  119.9 378.3 %all-reduce.6.cloned.1.call-start = ((), (), s32[]{:S(2)}) async-start(), calls=%async_computation.3 | async-start | bytes 16777216 | tf_op jit(solution)/shard_map/psum | solution.py:44
Sparse Core Ops, SparseCore 0:
  59.7 58.1 reduce-scatter.1
  124.0 123.9 all-reduce.3
  346.3 151.8 all-reduce.5
